TPU v7x, 32 devices: a whole 2x2x4 slice. The times are simulated.
32 devices in a mesh: groups: 2 (over x), lon: 16 (over z, y, core).
Axes of the slice: x: 2, y: 2, z: 4, core: 2. Of those that a mesh axis runs over, the one named last changes fastest.
Arguments:
- tracers: bfloat16 [2048, 64, 256], P(('groups', 'lon')), parts along dimension 0, may hold values from -6 to 6
- wind_fields: bfloat16 [2048, 64, 128], P(('groups', 'lon')), parts along dimension 0, may hold values from -3 to 3
- departures: int32 [32, 16, 2], P(('groups', 'lon')), parts along dimension 0, may hold values from -4 to 3, as said below
Outputs:
- advected: bfloat16 [2048, 64, 256], P(('groups', 'lon')), parts along dimension 0
There are 2 independent parts, one for each index of `groups`. A program takes and returns all parts, laid end to end along the dimension named above; each array names one. Nothing has to cross between parts.
Inputs may be any that keep to these rules, and one draw needn't show every extreme that they name: `departures`: entry 0 lies in -4..3 and entry 1 in -1..1 with q - entry 1 a valid band; in every sector exactly 4 bands share one value of entry 0, and no value is shared by more.
All inputs are finite; a program needn't handle non-finite values.
Results may differ from a plain program's by a relative error of at most 0.001.
Values may be sent and summed in bfloat16 or wider, within the bound.
A program may use at most 128 MiB of HBM per device.

v0:
```python
import jax
import jax.numpy as jnp
from jax import lax
from jax.sharding import PartitionSpec as P

CAP = 4
TRAJ = 3


CLIP_BOUND = 0.95


def with_halo(block, sides, width):
    for axis, dim in sides:
        count = lax.axis_size(axis)
        forward = [(i, i + 1) for i in range(count - 1)]
        forward.append((count - 1, 0))
        backward = [(target, source) for source, target in forward]
        low = lax.ppermute(
            lax.slice_in_dim(block, block.shape[dim] - width, None, axis=dim), axis, forward
        )
        high = lax.ppermute(lax.slice_in_dim(block, 0, width, axis=dim), axis, backward)
        block = jnp.concatenate([low, block, high], axis=dim)
    return block


def shifted(block, axis, distance):
    devices = range(lax.axis_size(axis))
    route = [((i - distance) % len(devices), i) for i in devices]
    return lax.ppermute(block, axis, route)


def linear_kernel(distance):
    return jnp.maximum(1.0 - jnp.abs(distance), 0.0)


def cubic_kernel(distance):
    magnitude = jnp.abs(distance)
    inner_part = 0.5 * (1.0 - magnitude) * (2.0 - magnitude) * (1.0 + magnitude)
    outer_part = -(magnitude - 1.0) * (2.0 - magnitude) * (3.0 - magnitude) / 6.0
    return jnp.where(magnitude < 1.0, inner_part, jnp.where(magnitude < 2.0, outer_part, 0.0))


def advect_tile(source_tile, arrival_wind):
    columns = source_tile.shape[0] - 4
    band_rows = source_tile.shape[1] - 4
    levels = arrival_wind.shape[-1] // 2
    tracer_ch = source_tile.shape[-1] - 4 * levels
    per_level = tracer_ch // levels
    wind_data = source_tile[:, :, tracer_ch:].astype(jnp.float32)
    extrapolated = 2.0 * wind_data[:, :, : 2 * levels] - wind_data[:, :, 2 * levels :]
    wind_here = arrival_wind.astype(jnp.float32)
    displace = jnp.clip(wind_here, -CLIP_BOUND, CLIP_BOUND)
    for iteration in range(TRAJ):
        lon_shift = displace[:, :, :levels]
        lat_shift = displace[:, :, levels:]
        accumulated = jnp.zeros_like(wind_here)
        for lat_step in (-1, 0, 1):
            lat_weight = linear_kernel(lat_step + lat_shift)
            for lon_step in (-1, 0, 1):
                weight = linear_kernel(lon_step + lon_shift) * lat_weight
                window = extrapolated[
                    2 + lon_step : 2 + lon_step + columns,
                    2 + lat_step : 2 + lat_step + band_rows,
                    :,
                ]
                accumulated = accumulated + jnp.concatenate([weight, weight], -1) * window
        displace = jnp.clip(0.5 * (wind_here + accumulated), -CLIP_BOUND, CLIP_BOUND)
    lon_shift = displace[:, :, :levels]
    lat_shift = displace[:, :, levels:]
    result = jnp.zeros((columns, band_rows, tracer_ch), jnp.float32)
    for lat_step in range(-2, 3):
        lat_dist = lat_step + lat_shift
        lat_weight = cubic_kernel(lat_dist)
        inner_rows = jnp.abs(lat_dist) < 1.0
        for lon_step in range(-2, 3):
            lon_dist = lon_step + lon_shift
            lon_weight = jnp.where(inner_rows, cubic_kernel(lon_dist), linear_kernel(lon_dist))
            weight = jnp.repeat(lon_weight * lat_weight, per_level, axis=-1)
            window = source_tile[
                2 + lon_step : 2 + lon_step + columns,
                2 + lat_step : 2 + lat_step + band_rows,
                :tracer_ch,
            ]
            result = result + weight * window.astype(jnp.float32)
    return result.astype(jnp.bfloat16)


def slot_bands(table_row, offset, capacity):
    matches = (table_row[:, 0] == offset).astype(jnp.int32)
    ordinal = jnp.cumsum(matches) - 1
    slot_index = jnp.arange(capacity, dtype=jnp.int32)
    picked = matches[None, :] * (ordinal[None, :] == slot_index[:, None]).astype(jnp.int32)
    band_ids = jnp.arange(table_row.shape[0], dtype=jnp.int32)
    return jnp.sum(picked * band_ids[None, :], axis=1)


def source_tiles(padded, table_row, offset, capacity, band_rows):
    chosen = slot_bands(table_row, offset, capacity)
    starts = (chosen - table_row[chosen, 1]) * band_rows

    def cut_tile(start_row):
        return lax.dynamic_slice_in_dim(padded, start_row, band_rows + 4, 1)

    return jax.vmap(cut_tile)(starts)


def on_device(tracers, wind_fields, departures):
    levels = wind_fields.shape[-1] // 4
    tracer_ch = tracers.shape[-1]
    columns = tracers.shape[0]
    band_count = departures.shape[1]
    band_rows = tracers.shape[1] // band_count
    capacity = CAP
    combined = jnp.concatenate([tracers, wind_fields], -1)
    combined = with_halo(combined, (("lon", 0),), 2)
    padded = jnp.concatenate(
        [combined[:, :1], combined[:, :1], combined, combined[:, -1:], combined[:, -1:]], 1
    )
    own_row = departures[0]
    table_rows = []
    for offset in range(-4, 4):
        if offset == 0:
            table_rows.append(own_row)
        else:
            table_rows.append(shifted(departures, "lon", -offset)[0])
    lon_tiles = own_row[:, 0]
    band_ids = jnp.arange(band_count, dtype=jnp.int32)
    earlier = (lon_tiles[:, None] == lon_tiles[None, :]) & (band_ids[None, :] < band_ids[:, None])
    position = (lon_tiles + 4) * capacity + jnp.sum(earlier.astype(jnp.int32), axis=1)
    arrival_all = wind_fields[:, :, : 2 * levels].reshape(
        columns, band_count, band_rows, 2 * levels
    )
    received = []
    for offset in range(-4, 4):
        outgoing = source_tiles(padded, table_rows[4 + offset], offset, capacity, band_rows)
        received.append(shifted(outgoing, "lon", offset))
    gathered = jnp.concatenate(received, 0)

    def advect_band(band_index):
        return advect_tile(gathered[position[band_index]], arrival_all[:, band_index])

    moved = lax.map(advect_band, band_ids)
    moved = jnp.transpose(moved, (1, 0, 2, 3))
    return moved.reshape(columns, band_count * band_rows, tracer_ch)


def solution(mesh):
    placed = (
        P(("groups", "lon"), None, None),
        P(("groups", "lon"), None, None),
        P(("groups", "lon"), None, None),
    )
    return jax.shard_map(
        on_device,
        mesh=mesh,
        in_specs=placed,
        out_specs=P(("groups", "lon"), None, None),
        check_vma=False,
    )
```

profile of v0, /device:TPU:0, one launch (start us, length us, event | category | flops | bytes accessed | tf_op | source)
XLA Modules:
  0.0 439.0 jit_solution(14753818186789090102)
XLA Ops:
  0.0 3.1 collective-permute-start.2
  6.0 3.7 collective-permute-start.11
  21.9 3.0 collective-permute-start.1
  30.3 3.1 constant_dynamic-update-slice_fusion.1
  34.6 3.0 gather_fusion.1
  39.0 3.0 gather_fusion.3
  44.0 3.0 gather_fusion.5
  52.9 3.0 gather_fusion.7
  59.1 3.0 gather_fusion.9
  63.5 13.5 %collective-permute-start.10 = (bf16[4,68,8,384]{3,2,1,0:T(8,128)(2,1)}, bf16[4,68,8,384]{3,2,1,0:T(8,128)(2,1)}, u32[]{:S(2)}, u32[]{:S(2)}) collective-permute-start(bf16[4,68,8,384]{3,2,1,0:T(8,128)(2,1)} %copy.64), channel_id=1, source_target_pairs={{0,0},{1,1},{2,2},{3,3},{4,4},{5,5},{6,6},{7,7},{8,8},{9,9},{10,10... | collective-permute-start | bytes 5013512 | tf_op jit(solution)/shard_map/ppermute | solution.py:30
  77.0 3.0 gather_fusion.11
  82.3 3.0 gather_fusion.13
  86.7 25.3 %collective-permute-done.5 = bf16[4,68,8,384]{3,2,1,0:T(8,128)(2,1)} collective-permute-done((bf16[4,68,8,384]{3,2,1,0:T(8,128)(2,1)}, bf16[4,68,8,384]{3,2,1,0:T(8,128)(2,1)}, u32[]{:S(2)}, u32[]{:S(2)}) %collective-permute-start.5) | collective-permute-done | bytes 1671200 | tf_op jit(solution)/shard_map/ppermute | solution.py:30
  114.2 3.0 gather_fusion.15
  118.6 28.6 %collective-permute-done.7 = bf16[4,68,8,384]{3,2,1,0:T(8,128)(2,1)} collective-permute-done((bf16[4,68,8,384]{3,2,1,0:T(8,128)(2,1)}, bf16[4,68,8,384]{3,2,1,0:T(8,128)(2,1)}, u32[]{:S(2)}, u32[]{:S(2)}) %collective-permute-start.7) | collective-permute-done | bytes 1671200 | tf_op jit(solution)/shard_map/ppermute | solution.py:30
  147.2 22.0 %collective-permute-start.16 = (bf16[4,68,8,384]{3,2,1,0:T(8,128)(2,1)}, bf16[4,68,8,384]{3,2,1,0:T(8,128)(2,1)S(1)}, u32[]{:S(2)}, u32[]{:S(2)}) collective-permute-start(bf16[4,68,8,384]{3,2,1,0:T(8,128)(2,1)} %copy.70), channel_id=1, source_target_pairs={{13,0},{14,1},{15,2},{0,3},{1,4},{2,5},{3,6},{4,7},{5,8},{6,9},{7,... | collective-permute-start | bytes 5013512 | tf_op jit(solution)/shard_map/ppermute | solution.py:30
  171.1 2.8 constant_dynamic-update-slice_fusion.9
  179.5 2.8 constant_dynamic-update-slice_fusion.6
  185.1 2.9 constant_dynamic-update-slice_fusion.4
  188.0 14.2 %collective-permute-done.14 = bf16[4,68,8,384]{3,2,1,0:T(8,128)(2,1)} collective-permute-done((bf16[4,68,8,384]{3,2,1,0:T(8,128)(2,1)}, bf16[4,68,8,384]{3,2,1,0:T(8,128)(2,1)}, u32[]{:S(2)}, u32[]{:S(2)}) %collective-permute-start.14) | collective-permute-done | bytes 1671200 | tf_op jit(solution)/shard_map/ppermute | solution.py:30
  205.0 18.3 %collective-permute-done.16 = bf16[4,68,8,384]{3,2,1,0:T(8,128)(2,1)S(1)} collective-permute-done((bf16[4,68,8,384]{3,2,1,0:T(8,128)(2,1)}, bf16[4,68,8,384]{3,2,1,0:T(8,128)(2,1)S(1)}, u32[]{:S(2)}, u32[]{:S(2)}) %collective-permute-start.16) | collective-permute-done | bytes 1671200 | tf_op jit(solution)/shard_map/ppermute | solution.py:30
  224.7 208.6 %while.13 = (s32[]{:T(128)}, bf16[16,64,4,256]{1,3,2,0:T(8,128)(2,1)}, s32[16]{0:T(128)S(1)}, bf16[64,16,4,64]{3,0,2,1:T(8,128)(2,1)}, s32[16]{0:T(128)S(1)}, /*...) while((s32[]{:T(128)}, bf16[16,64,4,256]{1,3,2,0:T(8,128)(2,1)}, ...), condition=%wide.region_18.19_spmd, body=%wide.region_17.18_spmd.sunk | while | flops 11304968 | bytes 12288713 | solution.py:143
  404.4 2.8 bitcast_dynamic-update-slice_fusion.2
  433.3 5.6 %copy.74 = bf16[64,64,256]{2,1,0:T(8,128)(2,1)} copy(bf16[64,64,256]{0,2,1:T(8,128)(2,1)} %bitcast.80) | data formatting | bytes 4194304 | tf_op jit(solution)/shard_map/reshape | solution.py:145
  (445 shorter events, 199.1 us)
Async XLA Ops:
  0.0 15.9 %copy-start = (s32[1,16,2]{1,2,0:T(2,128)S(1)}, s32[1,16,2]{1,2,0:T(2,128)}, u32[]{:S(2)}) copy-start(s32[1,16,2]{1,2,0:T(2,128)} %param.7) | copy-start | bytes 388
  0.0 13.9 %copy-start.1 = (bf16[64,64,128]{2,1,0:T(8,128)(2,1)S(1)}, bf16[64,64,128]{2,1,0:T(8,128)(2,1)}, u32[]{:S(2)}) copy-start(bf16[64,64,128]{2,1,0:T(8,128)(2,1)} %param.6) | copy-start | bytes 3145732
  0.0 16.6 %collective-permute-start.2 = (s32[1,16,2]{1,2,0:T(2,128)}, s32[1,16,2]{1,2,0:T(2,128)S(1)}, u32[]{:S(2)}, u32[]{:S(2)}) collective-permute-start(s32[1,16,2]{1,2,0:T(2,128)} %param.7), channel_id=1, source_target_pairs={{12,0},{13,1},{14,2},{15,3},{0,4},{1,5},{2,6},{3,7},{4,8},{5,9},{6... | collective-permute-start | bytes 392 | tf_op jit(solution)/shard_map/ppermute | solution.py:30
  3.1 15.1 %collective-permute-start.4 = (s32[1,16,2]{1,2,0:T(2,128)}, s32[1,16,2]{1,2,0:T(2,128)S(1)}, u32[]{:S(2)}, u32[]{:S(2)}) collective-permute-start(s32[1,16,2]{1,2,0:T(2,128)} %param.7), channel_id=1, source_target_pairs={{13,0},{14,1},{15,2},{0,3},{1,4},{2,5},{3,6},{4,7},{5,8},{6,9},{7,... | collective-permute-start | bytes 392 | tf_op jit(solution)/shard_map/ppermute | solution.py:30
  3.7 15.6 %collective-permute-start.6 = (s32[1,16,2]{1,2,0:T(2,128)}, s32[1,16,2]{1,2,0:T(2,128)S(1)}, u32[]{:S(2)}, u32[]{:S(2)}) collective-permute-start(s32[1,16,2]{1,2,0:T(2,128)} %param.7), channel_id=1, source_target_pairs={{14,0},{15,1},{0,2},{1,3},{2,4},{3,5},{4,6},{5,7},{6,8},{7,9},{8,1... | collective-permute-start | bytes 392 | tf_op jit(solution)/shard_map/ppermute | solution.py:30
  5.3 16.6 %collective-permute-start.8 = (s32[1,16,2]{1,2,0:T(2,128)}, s32[1,16,2]{1,2,0:T(2,128)S(1)}, u32[]{:S(2)}, u32[]{:S(2)}) collective-permute-start(s32[1,16,2]{1,2,0:T(2,128)} %param.7), channel_id=1, source_target_pairs={{15,0},{0,1},{1,2},{2,3},{3,4},{4,5},{5,6},{6,7},{7,8},{8,9},{9,10... | collective-permute-start | bytes 392 | tf_op jit(solution)/shard_map/ppermute | solution.py:30
  6.0 19.3 %collective-permute-start.11 = (s32[1,16,2]{1,2,0:T(2,128)}, s32[1,16,2]{1,2,0:T(2,128)S(1)}, u32[]{:S(2)}, u32[]{:S(2)}) collective-permute-start(s32[1,16,2]{1,2,0:T(2,128)} %param.7), channel_id=1, source_target_pairs={{1,0},{2,1},{3,2},{4,3},{5,4},{6,5},{7,6},{8,7},{9,8},{10,9},{11,1... | collective-permute-start | bytes 392 | tf_op jit(solution)/shard_map/ppermute | solution.py:30
  16.6 8.9 %collective-permute-start.13 = (s32[1,16,2]{1,2,0:T(2,128)S(1)}, s32[1,16,2]{1,2,0:T(2,128)S(1)}, u32[]{:S(2)}, u32[]{:S(2)}) collective-permute-start(s32[1,16,2]{1,2,0:T(2,128)S(1)} %copy-done), channel_id=1, source_target_pairs={{2,0},{3,1},{4,2},{5,3},{6,4},{7,5},{8,6},{9,7},{10,8},{11,9},{12,... | collective-permute-start | bytes 392 | tf_op jit(solution)/shard_map/ppermute | solution.py:30
  18.2 34.6 %collective-permute-start.15 = (s32[1,16,2]{1,2,0:T(2,128)S(1)}, s32[1,16,2]{1,2,0:T(2,128)S(1)}, u32[]{:S(2)}, u32[]{:S(2)}) collective-permute-start(s32[1,16,2]{1,2,0:T(2,128)S(1)} %copy-done), channel_id=1, source_target_pairs={{3,0},{4,1},{5,2},{6,3},{7,4},{8,5},{9,6},{10,7},{11,8},{12,9},{13... | collective-permute-start | bytes 392 | tf_op jit(solution)/shard_map/ppermute | solution.py:30
  19.3 7.1 %collective-permute-start = (bf16[2,64,384]{2,0,1:T(2,128)(2,1)}, bf16[2,64,384]{2,0,1:T(2,128)(2,1)S(1)}, u32[]{:S(2)}, u32[]{:S(2)}) collective-permute-start(bf16[2,64,384]{2,0,1:T(2,128)(2,1)} %get-tuple-element.218), channel_id=1, source_target_pairs={{0,1},{1,2},{2,3},{3,4},{4,5},{5,6},{6,7},{7,8},{8,9},{9,10},{10,1... | collective-permute-start | bytes 294920 | tf_op jit(solution)/shard_map/ppermute | solution.py:19
  21.9 5.2 %collective-permute-start.1 = (bf16[2,64,384]{2,0,1:T(2,128)(2,1)S(1)}, bf16[2,64,384]{2,0,1:T(2,128)(2,1)S(1)}, u32[]{:S(2)}, u32[]{:S(2)}) collective-permute-start(bf16[2,64,384]{2,0,1:T(2,128)(2,1)S(1)} %get-tuple-element.219), channel_id=1, source_target_pairs={{1,0},{2,1},{3,2},{4,3},{5,4},{6,5},{7,6},{8,7},{9,8},{10,9},{11,1... | collective-permute-start | bytes 294920 | tf_op jit(solution)/shard_map/ppermute | solution.py:22
  39.0 42.6 %collective-permute-start.3 = (bf16[4,68,8,384]{3,2,1,0:T(8,128)(2,1)}, bf16[4,68,8,384]{3,2,1,0:T(8,128)(2,1)S(1)}, u32[]{:S(2)}, u32[]{:S(2)}) collective-permute-start(bf16[4,68,8,384]{3,2,1,0:T(8,128)(2,1)} %copy.56), channel_id=1, source_target_pairs={{4,0},{5,1},{6,2},{7,3},{8,4},{9,5},{10,6},{11,7},{12,8},{13,9},{1... | collective-permute-start | bytes 5013512 | tf_op jit(solution)/shard_map/ppermute | solution.py:30
  43.4 68.6 %collective-permute-start.5 = (bf16[4,68,8,384]{3,2,1,0:T(8,128)(2,1)}, bf16[4,68,8,384]{3,2,1,0:T(8,128)(2,1)}, u32[]{:S(2)}, u32[]{:S(2)}) collective-permute-start(bf16[4,68,8,384]{3,2,1,0:T(8,128)(2,1)} %copy.58), channel_id=1, source_target_pairs={{3,0},{4,1},{5,2},{6,3},{7,4},{8,5},{9,6},{10,7},{11,8},{12,9},{13... | collective-permute-start | bytes 5013512 | tf_op jit(solution)/shard_map/ppermute | solution.py:30
  48.4 98.8 %collective-permute-start.7 = (bf16[4,68,8,384]{3,2,1,0:T(8,128)(2,1)}, bf16[4,68,8,384]{3,2,1,0:T(8,128)(2,1)}, u32[]{:S(2)}, u32[]{:S(2)}) collective-permute-start(bf16[4,68,8,384]{3,2,1,0:T(8,128)(2,1)} %copy.60), channel_id=1, source_target_pairs={{2,0},{3,1},{4,2},{5,3},{6,4},{7,5},{8,6},{9,7},{10,8},{11,9},{12,... | collective-permute-start | bytes 5013512 | tf_op jit(solution)/shard_map/ppermute | solution.py:30
  57.3 122.2 %collective-permute-start.9 = (bf16[4,68,8,384]{3,2,1,0:T(8,128)(2,1)}, bf16[4,68,8,384]{3,2,1,0:T(8,128)(2,1)}, u32[]{:S(2)}, u32[]{:S(2)}) collective-permute-start(bf16[4,68,8,384]{3,2,1,0:T(8,128)(2,1)} %copy.62), channel_id=1, source_target_pairs={{1,0},{2,1},{3,2},{4,3},{5,4},{6,5},{7,6},{8,7},{9,8},{10,9},{11,1... | collective-permute-start | bytes 5013512 | tf_op jit(solution)/shard_map/ppermute | solution.py:30
  63.5 118.8 %collective-permute-start.10 = (bf16[4,68,8,384]{3,2,1,0:T(8,128)(2,1)}, bf16[4,68,8,384]{3,2,1,0:T(8,128)(2,1)}, u32[]{:S(2)}, u32[]{:S(2)}) collective-permute-start(bf16[4,68,8,384]{3,2,1,0:T(8,128)(2,1)} %copy.64), channel_id=1, source_target_pairs={{0,0},{1,1},{2,2},{3,3},{4,4},{5,5},{6,6},{7,7},{8,8},{9,9},{10,10... | collective-permute-start | bytes 5013512 | tf_op jit(solution)/shard_map/ppermute | solution.py:30
  81.5 5.2 %copy-start.3 = (bf16[4,68,8,384]{3,2,1,0:T(8,128)(2,1)}, bf16[4,68,8,384]{3,2,1,0:T(8,128)(2,1)S(1)}, u32[]{:S(2)}) copy-start(bf16[4,68,8,384]{3,2,1,0:T(8,128)(2,1)S(1)} %collective-permute-done.3) | copy-start | bytes 5013508
  81.5 103.6 %collective-permute-start.12 = (bf16[4,68,8,384]{3,2,1,0:T(8,128)(2,1)}, bf16[4,68,8,384]{3,2,1,0:T(8,128)(2,1)}, u32[]{:S(2)}, u32[]{:S(2)}) collective-permute-start(bf16[4,68,8,384]{3,2,1,0:T(8,128)(2,1)} %copy.66), channel_id=1, source_target_pairs={{15,0},{0,1},{1,2},{2,3},{3,4},{4,5},{5,6},{6,7},{7,8},{8,9},{9,10... | collective-permute-start | bytes 5013512 | tf_op jit(solution)/shard_map/ppermute | solution.py:30
  86.7 82.5 %copy-start.2 = (bf16[64,64,128]{2,1,0:T(8,128)(2,1)S(1)}, bf16[64,64,128]{2,1,0:T(8,128)(2,1)}, u32[]{:S(2)}) copy-start(bf16[64,64,128]{2,1,0:T(8,128)(2,1)} %param.6) | copy-start | bytes 3145732
  112.0 90.2 %collective-permute-start.14 = (bf16[4,68,8,384]{3,2,1,0:T(8,128)(2,1)}, bf16[4,68,8,384]{3,2,1,0:T(8,128)(2,1)}, u32[]{:S(2)}, u32[]{:S(2)}) collective-permute-start(bf16[4,68,8,384]{3,2,1,0:T(8,128)(2,1)} %copy.68), channel_id=1, source_target_pairs={{14,0},{15,1},{0,2},{1,3},{2,4},{3,5},{4,6},{5,7},{6,8},{7,9},{8,1... | collective-permute-start | bytes 5013512 | tf_op jit(solution)/shard_map/ppermute | solution.py:30
  147.2 76.0 %collective-permute-start.16 = (bf16[4,68,8,384]{3,2,1,0:T(8,128)(2,1)}, bf16[4,68,8,384]{3,2,1,0:T(8,128)(2,1)S(1)}, u32[]{:S(2)}, u32[]{:S(2)}) collective-permute-start(bf16[4,68,8,384]{3,2,1,0:T(8,128)(2,1)} %copy.70), channel_id=1, source_target_pairs={{13,0},{14,1},{15,2},{0,3},{1,4},{2,5},{3,6},{4,7},{5,8},{6,9},{7,... | collective-permute-start | bytes 5013512 | tf_op jit(solution)/shard_map/ppermute | solution.py:30
where the time goes:
time: 443 us; the launch traced here: 439 us
  local copies, waits for them, and re-layouts  135 us (30%)
  other arithmetic  95.1 us (21%)
  waiting for transfers between devices  87.6 us (20%)
  loops' own time  63.9 us (14%)
  starting transfers between devices  57.2 us (13%)
    ppermute x15, waiting for transfers between devices, shifted(): return lax.ppermute(block, axis, route)  86.4 us
    another operation x1, loops' own time, on_device(): moved = lax.map(advect_band, band_ids)  63.9 us
    ppermute x15, starting transfers between devices, shifted(): return lax.ppermute(block, axis, route)  52.6 us
    dynamic_update_slice x16, other arithmetic, on_device(): moved = lax.map(advect_band, band_ids)  44.7 us
    gather x16, local copies, waits for them, and re-layouts, cut_tile(): return lax.dynamic_slice_in_dim(padded, start_row, band_rows + 4, 1)  35.3 us
    unnamed x21, local copies, waits for them, and re-layouts  26 us
    dynamic_slice x32, local copies, waits for them, and re-layouts, advect_band(): gathered[position[band_index]]  24.6 us
    min x48, other arithmetic, advect_tile(): jnp.clip(0.5 * (wind_here + accumulated), -CLIP_BOUND, CLIP_BOUND)  18.1 us
  transfers between devices with their start and end apart: 17, of which 6 were waited for; matrix products, arithmetic and copies ran while one was open for 18% of the time, Pallas kernels for 0%

commit v1 on v0

v1 whole, which is shorter than its diff:
```python
import functools

import jax
import jax.numpy as jnp
from jax import lax
from jax.experimental import pallas as pl
from jax.experimental.pallas import tpu as pltpu
from jax.sharding import PartitionSpec as P

CAP = 4
TRAJ = 3
CLIP_BOUND = 0.95
LOW, HIGH = -3, 4
CHUNKS = 8
MESH = pl.DeviceIdType.MESH


def linear_kernel(distance):
    return jnp.maximum(1.0 - jnp.abs(distance), 0.0)


def linear_near(r):
    return [jnp.maximum(r, 0.0), 1.0 - jnp.abs(r), jnp.maximum(-r, 0.0)]


def cubic_all(r):
    t = jnp.abs(r)
    u = 1.0 - t
    v = 1.0 + t
    w = 2.0 - t
    uw = u * w
    tv = t * v
    near0 = 0.5 * (uw * v)
    near1 = 0.5 * (tv * w)
    far1 = (-1.0 / 6.0) * (uw * t)
    far2 = (-1.0 / 6.0) * (tv * u)
    pos = r > 0.0
    zero = jnp.zeros_like(t)
    return [
        jnp.where(pos, far2, zero),
        jnp.where(pos, near1, far1),
        near0,
        jnp.where(pos, far1, near1),
        jnp.where(pos, zero, far2),
    ]


def place(dep_ref, band, rows, total_rows):
    source = band - dep_ref[band, 1]
    first = source * rows - 2
    base = jnp.clip((first + 8) // 8 * 8 - 8, 0, total_rows - 16)
    return base, first - base


def advect_kernel(columns, rows, levels, dep_ref, here_ref, wt_ref, ww_ref, out_ref,
                  tbuf, wbuf, t8, w8, s_ref, p_ref, r_ref, d_ref, e_ref, sems):
    g = pl.program_id(0)
    steps = pl.num_programs(0)
    total_rows = wt_ref.shape[1]
    width = columns + 4
    tracer_ch = wt_ref.shape[2]
    lane_tiles = tracer_ch // 128
    half = columns // 2
    slot = lax.rem(g, 2)

    def copies(step, where, j):
        band = step * 2 + j
        base, _ = place(dep_ref, band, rows, total_rows)
        start = (HIGH - 1 - dep_ref[band, 0]) * columns
        at = (pl.ds(start, width), pl.ds(pl.multiple_of(base, 8), 16), slice(None))
        return (
            pltpu.make_async_copy(wt_ref.at[at], tbuf.at[where, j], sems.at[where, j, 0]),
            pltpu.make_async_copy(ww_ref.at[at], wbuf.at[where, j], sems.at[where, j, 1]),
        )

    @pl.when(g == 0)
    def _():
        for j in range(2):
            for c in copies(0, 0, j):
                c.start()
        row = lax.broadcasted_iota(jnp.int32, e_ref.shape, 0)
        col = lax.broadcasted_iota(jnp.int32, e_ref.shape, 1)
        part = col // tracer_ch
        level = (col % tracer_ch) // (tracer_ch // levels)
        hit = (row % 128) == part * levels + level
        e_ref[...] = jnp.where(hit, 1.0, 0.0).astype(e_ref.dtype)

    @pl.when(g + 1 < steps)
    def _():
        for j in range(2):
            for c in copies(g + 1, 1 - slot, j):
                c.start()

    for j in range(2):
        for c in copies(g, slot, j):
            c.wait()

    def cut(x, off):
        if off < 0:
            return jnp.concatenate([x[:, :1]] * (-off) + [x[:, : 8 + off]], axis=1)
        if off + 8 > 16:
            return jnp.concatenate([x[:, off:]] + [x[:, 15:]] * (off - 8), axis=1)
        return x[:, off : off + 8]

    for j in range(2):
        _, offset = place(dep_ref, g * 2 + j, rows, total_rows)
        for off in (-2, 2, 6, 10):

            @pl.when(offset == off)
            def _(j=j, off=off):
                def move(i, carry):
                    cs = pl.ds(i * 4, 4)
                    t8[j, cs] = cut(tbuf[slot, j, cs].astype(jnp.float32), off)
                    w8[j, cs] = cut(wbuf[slot, j, cs].astype(jnp.float32), off)
                    return carry

                lax.fori_loop(0, width // 4, move, 0)

    def interleave(a, b, ks):
        sub = lax.broadcasted_iota(jnp.int32, a.shape, a.ndim - 2)
        b = pltpu.roll(b, 4, a.ndim - 2)
        for k in ks:
            e = jnp.where((sub + 8 - k) % 8 < 4, a, b)
            yield k, (pltpu.roll(e, 8 - k, a.ndim - 2) if k else e)

    def build(i, carry):
        for u in range(2):
            col = i * 2 + u
            for k, value in interleave(t8[0, col], t8[1, col], range(5)):
                s_ref[k, col] = value
        return carry

    lax.fori_loop(0, width // 2, build, 0)

    def packed_ext(j, col):
        low = w8[j, col]
        high = w8[j, col + half]
        lane = lax.broadcasted_iota(jnp.int32, low.shape, 1)
        return jnp.where(
            lane < 64, 2.0 * low - pltpu.roll(low, 64, 1), 2.0 * pltpu.roll(high, 64, 1) - high
        )

    def build_winds(i, carry):
        for u in range(2):
            col = 1 + i * 2 + u
            for k, value in interleave(packed_ext(0, col), packed_ext(1, col), range(1, 4)):
                p_ref[k - 1, col] = value
        return carry

    lax.fori_loop(0, (half + 2) // 2, build_winds, 0)

    block = 8

    def trace(i, carry):
        first = i * block
        low = here_ref[pl.ds(first, block)].astype(jnp.float32)
        high = here_ref[pl.ds(first + half, block)].astype(jnp.float32)
        lane = lax.broadcasted_iota(jnp.int32, low.shape, 2)
        east = (lane % 64) < 32
        here = jnp.where(lane < 64, low, pltpu.roll(high, 64, 2))
        d = jnp.clip(here, -CLIP_BOUND, CLIP_BOUND)
        for _ in range(TRAJ):
            swapped = jnp.where(east, pltpu.roll(d, 96, 2), pltpu.roll(d, 32, 2))
            lon = linear_near(jnp.where(east, d, swapped))
            lat = linear_near(jnp.where(east, swapped, d))
            acc = None
            for b in range(3):
                line = None
                for a in range(3):
                    term = lon[a] * p_ref[b, pl.ds(first + 1 + a, block)]
                    line = term if line is None else line + term
                line = lat[b] * line
                acc = line if acc is None else acc + line
            d = jnp.clip(0.5 * (here + acc), -CLIP_BOUND, CLIP_BOUND)
        hi = d.astype(jnp.bfloat16).astype(jnp.float32)
        d_ref[pl.ds(first, block), :, :128] = hi
        d_ref[pl.ds(first, block), :, 128:] = d - hi
        return carry

    lax.fori_loop(0, half // block, trace, 0)

    both = d_ref[...].reshape(half * 8, 256).astype(jnp.bfloat16)
    for part in range(4):
        at = slice(part * tracer_ch, (part + 1) * tracer_ch)
        r_ref[:, :, at] = jnp.dot(
            both, e_ref[:, at], preferred_element_type=jnp.float32
        ).reshape(half, 8, tracer_ch)

    def interpolate(i, carry):
        for h in range(2):
            for v in range(lane_tiles):
                lanes = slice(v * 128, (v + 1) * 128)
                re = r_ref[i, :, (2 * h) * tracer_ch + v * 128 : (2 * h) * tracer_ch + (v + 1) * 128]
                rn = r_ref[i, :, (2 * h + 1) * tracer_ch + v * 128 : (2 * h + 1) * tracer_ch + (v + 1) * 128]
                cubic = cubic_all(re)
                linear = [linear_kernel(re - 2.0)] + linear_near(re) + [linear_kernel(re + 2.0)]
                lat = cubic_all(rn)
                inner = {-1: rn > 0.0, 1: rn < 0.0}
                acc = None
                for b in range(-2, 3):
                    line = None
                    for a in range(5):
                        if b == 0:
                            weight = cubic[a]
                        elif abs(b) == 2:
                            weight = linear[a]
                        else:
                            weight = jnp.where(inner[b], cubic[a], linear[a])
                        term = weight * s_ref[b + 2, i + half * h + a, :, lanes]
                        line = term if line is None else line + term
                    line = lat[b + 2] * line
                    acc = line if acc is None else acc + line
                out_ref[i + half * h, :, lanes] = acc.astype(out_ref.dtype)
        return carry

    lax.fori_loop(0, half, interpolate, 0)


def advect(tracers_shape, wind_fields, departures, wt, ww):
    columns, total_rows, tracer_ch = tracers_shape
    levels = wind_fields.shape[-1] // 4
    bands = departures.shape[1]
    rows = total_rows // bands
    width = columns + 4
    half = columns // 2
    f32 = jnp.float32
    return pl.pallas_call(
        functools.partial(advect_kernel, columns, rows, levels),
        out_shape=jax.ShapeDtypeStruct(tracers_shape, jnp.bfloat16),
        grid_spec=pltpu.PrefetchScalarGridSpec(
            num_scalar_prefetch=1,
            grid=(bands // 2,),
            in_specs=[
                pl.BlockSpec((columns, 8, 4 * levels), lambda g, dep: (0, g, 0)),
                pl.BlockSpec(memory_space=pl.ANY),
                pl.BlockSpec(memory_space=pl.ANY),
            ],
            out_specs=pl.BlockSpec((columns, 8, tracer_ch), lambda g, dep: (0, g, 0)),
            scratch_shapes=[
                pltpu.VMEM((2, 2, width, 16, tracer_ch), jnp.bfloat16),
                pltpu.VMEM((2, 2, width, 16, 4 * levels), jnp.bfloat16),
                pltpu.VMEM((2, width, 8, tracer_ch), f32),
                pltpu.VMEM((2, width, 8, 4 * levels), f32),
                pltpu.VMEM((5, width, 8, tracer_ch), f32),
                pltpu.VMEM((3, half + 4, 8, 4 * levels), f32),
                pltpu.VMEM((half, 8, 4 * tracer_ch), f32),
                pltpu.VMEM((half, 8, 256), f32),
                pltpu.VMEM((256, 4 * tracer_ch), jnp.bfloat16),
                pltpu.SemaphoreType.DMA((2, 2, 2)),
            ],
        ),
        compiler_params=pltpu.CompilerParams(vmem_limit_bytes=40 * 1024 * 1024),
        name="advect",
    )(departures[0], wind_fields, wt, ww)

def shifted(block, distance):
    count = lax.axis_size("lon")
    route = [((i - distance) % count, i) for i in range(count)]
    return lax.ppermute(block, "lon", route)


def window(block):
    pieces = [shifted(block[-2:], -LOW + 1)]
    for offset in range(LOW, HIGH + 1):
        pieces.append(block if offset == 0 else shifted(block, -offset))
    pieces.append(shifted(block[:2], -HIGH - 1))
    return jnp.concatenate(pieces, 0)


def on_device(tracers, wind_fields, departures):
    return advect(tracers.shape, wind_fields, departures, window(tracers), window(wind_fields))


def solution(mesh):
    placed = P(("groups", "lon"), None, None)
    return jax.shard_map(
        on_device,
        mesh=mesh,
        in_specs=(placed, placed, placed),
        out_specs=placed,
        check_vma=False,
    )
```

time: 443 us -> 405 us (0.914)
  waiting for transfers between devices: 87.6 us -> 205 us
  local copies, waits for them, and re-layouts: 135 us -> 26.3 us
  other arithmetic: 95.1 us -> 0 us
  loops' own time: 63.9 us -> 0 us
  starting transfers between devices: 57.2 us -> 118 us
  Pallas kernels: 0 us -> 55 us
    ppermute x17 -> x18, waiting for transfers between devices: 87.6 us -> 205 us  [shifted(): return lax.ppermute(block, 'lon', route)]
    another operation x1 -> x0, loops' own time: 63.9 us -> none  [on_device(): moved = lax.map(advect_band, band_ids)]
    ppermute x17 -> x18, starting transfers between devices: 57.2 us -> 118 us  [shifted(): return lax.ppermute(block, 'lon', route)]
    dynamic_slice x96 -> x0, local copies, waits for them, and re-layouts: 58.6 us -> none  [the longest x32 24.6 us: advect_band(): gathered[position[band_index]]]
    pallas_call x0 -> x1, Pallas kernels: none -> 55 us  [advect(): pl.pallas_call(functools.partial(advect_kernel, columns, rows, levels), o...]
    dynamic_update_slice x16 -> x0, other arithmetic: 44.7 us -> none  [on_device(): moved = lax.map(advect_band, band_ids)]
    gather x24 -> x0, local copies, waits for them, and re-layouts: 40.5 us -> none  [the longest x16 35.3 us: cut_tile(): return lax.dynamic_slice_in_dim(padded, start_row, band_rows + 4, 1)]
    mul x112 -> x0, other arithmetic: 22 us -> none  [the longest x64 17.8 us: advect_tile(): weight = jnp.repeat(lon_weight * lat_weight, per_level, axis=-1)]
  transfers between devices with their start and end apart: 17 -> 18, of which waited for: 6 -> 8; matrix products, arithmetic and copies ran while one was open for 18% -> 6% of each run, Pallas kernels for 0% -> 0%
where the time goes in v1:
time: 405 us
  waiting for transfers between devices  205 us (51%)
  starting transfers between devices  118 us (29%)
  Pallas kernels  55 us (14%)
  local copies, waits for them, and re-layouts  26.3 us (6%)
    ppermute x18, waiting for transfers between devices, shifted(): return lax.ppermute(block, 'lon', route)  205 us
    ppermute x18, starting transfers between devices, shifted(): return lax.ppermute(block, 'lon', route)  118 us
    pallas_call x1, Pallas kernels, advect(): pl.pallas_call(functools.partial(advect_kernel, columns, rows, levels), o...  55 us
    unnamed x30, local copies, waits for them, and re-layouts  23.2 us
  transfers between devices with their start and end apart: 18, of which 8 were waited for; matrix products, arithmetic and copies ran while one was open for 6% of the time, Pallas kernels for 0%

profile of v1, /device:TPU:0, one launch (start us, length us, event | category | flops | bytes accessed | tf_op | source)
XLA Modules:
  0.0 404.7 jit_solution(8890050741924940837)
XLA Ops:
  0.0 2.4 collective-permute-start.10
  2.4 1.5 collective-permute-start.11
  4.8 1.6 collective-permute-start.9
  6.5 4.3 %collective-permute-start.13 = (bf16[64,64,128]{2,1,0:T(8,128)(2,1)}, bf16[64,64,128]{2,1,0:T(8,128)(2,1)S(1)}, u32[]{:S(2)}, u32[]{:S(2)}) collective-permute-start(bf16[64,64,128]{2,1,0:T(8,128)(2,1)} %here_ref.1), channel_id=1, source_target_pairs={{1,0},{2,1},{3,2},{4,3},{5,4},{6,5},{7,6},{8,7},{9,8},{10,9},{11,1... | collective-permute-start | bytes 3145736 | tf_op jit(solution)/shard_map/ppermute | solution.py:259
  10.8 42.9 %collective-permute-start.17 = (bf16[2,64,128]{2,1,0:T(8,128)(2,1)S(1)}, bf16[2,64,128]{2,1,0:T(8,128)(2,1)S(1)}, u32[]{:S(2)}, u32[]{:S(2)}) collective-permute-start(bf16[2,64,128]{2,1,0:T(8,128)(2,1)S(1)} %get-tuple-element.7), channel_id=1, source_target_pairs={{5,0},{6,1},{7,2},{8,3},{9,4},{10,5},{11,6},{12,7},{13,8},{14,9},{... | collective-permute-start | bytes 98312 | tf_op jit(solution)/shard_map/ppermute | solution.py:259
  55.3 1.7 collective-permute-start
  57.0 4.4 %collective-permute-done = bf16[2,64,256]{2,1,0:T(8,128)(2,1)S(1)} collective-permute-done((bf16[2,64,256]{2,1,0:T(8,128)(2,1)S(1)}, bf16[2,64,256]{2,1,0:T(8,128)(2,1)S(1)}, u32[]{:S(2)}, u32[]{:S(2)}) %collective-permute-start) | collective-permute-done | bytes 65568 | tf_op jit(solution)/shard_map/ppermute | solution.py:259
  61.4 6.2 %collective-permute-start.1 = (bf16[64,64,256]{2,1,0:T(8,128)(2,1)}, bf16[64,64,256]{2,1,0:T(8,128)(2,1)S(1)}, u32[]{:S(2)}, u32[]{:S(2)}) collective-permute-start(bf16[64,64,256]{2,1,0:T(8,128)(2,1)} %param.3), channel_id=1, source_target_pairs={{13,0},{14,1},{15,2},{0,3},{1,4},{2,5},{3,6},{4,7},{5,8},{6,9},{7,... | collective-permute-start | bytes 6291464 | tf_op jit(solution)/shard_map/ppermute | solution.py:259
  67.6 4.1 %collective-permute-start.2 = (bf16[64,64,256]{2,1,0:T(8,128)(2,1)}, bf16[64,64,256]{2,1,0:T(8,128)(2,1)}, u32[]{:S(2)}, u32[]{:S(2)}) collective-permute-start(bf16[64,64,256]{2,1,0:T(8,128)(2,1)} %param.3), channel_id=1, source_target_pairs={{14,0},{15,1},{0,2},{1,3},{2,4},{3,5},{4,6},{5,7},{6,8},{7,9},{8,1... | collective-permute-start | bytes 6291464 | tf_op jit(solution)/shard_map/ppermute | solution.py:259
  71.7 2.5 collective-permute-start.14
  75.0 45.1 %collective-permute-done.14 = bf16[64,64,128]{2,1,0:T(8,128)(2,1)S(1)} collective-permute-done((bf16[64,64,128]{2,1,0:T(8,128)(2,1)}, bf16[64,64,128]{2,1,0:T(8,128)(2,1)S(1)}, u32[]{:S(2)}, u32[]{:S(2)}) %collective-permute-start.14) | collective-permute-done | bytes 1048608 | tf_op jit(solution)/shard_map/ppermute | solution.py:259
  120.1 12.8 %collective-permute-start.3 = (bf16[64,64,256]{2,1,0:T(8,128)(2,1)}, bf16[64,64,256]{2,1,0:T(8,128)(2,1)}, u32[]{:S(2)}, u32[]{:S(2)}) collective-permute-start(bf16[64,64,256]{2,1,0:T(8,128)(2,1)} %param.3), channel_id=1, source_target_pairs={{15,0},{0,1},{1,2},{2,3},{3,4},{4,5},{5,6},{6,7},{7,8},{8,9},{9,10... | collective-permute-start | bytes 6291464 | tf_op jit(solution)/shard_map/ppermute | solution.py:259
  133.7 40.5 %collective-permute-done.15 = bf16[64,64,128]{2,1,0:T(8,128)(2,1)} collective-permute-done((bf16[64,64,128]{2,1,0:T(8,128)(2,1)}, bf16[64,64,128]{2,1,0:T(8,128)(2,1)}, u32[]{:S(2)}, u32[]{:S(2)}) %collective-permute-start.15) | collective-permute-done | bytes 1048608 | tf_op jit(solution)/shard_map/ppermute | solution.py:259
  174.3 14.4 %collective-permute-start.4 = (bf16[64,64,256]{2,1,0:T(8,128)(2,1)}, bf16[64,64,256]{2,1,0:T(8,128)(2,1)S(1)}, u32[]{:S(2)}, u32[]{:S(2)}) collective-permute-start(bf16[64,64,256]{2,1,0:T(8,128)(2,1)} %param.3), channel_id=1, source_target_pairs={{1,0},{2,1},{3,2},{4,3},{5,4},{6,5},{7,6},{8,7},{9,8},{10,9},{11,1... | collective-permute-start | bytes 6291464 | tf_op jit(solution)/shard_map/ppermute | solution.py:259
  188.7 23.0 %collective-permute-start.5 = (bf16[64,64,256]{2,1,0:T(8,128)(2,1)}, bf16[64,64,256]{2,1,0:T(8,128)(2,1)S(1)}, u32[]{:S(2)}, u32[]{:S(2)}) collective-permute-start(bf16[64,64,256]{2,1,0:T(8,128)(2,1)} %param.3), channel_id=1, source_target_pairs={{2,0},{3,1},{4,2},{5,3},{6,4},{7,5},{8,6},{9,7},{10,8},{11,9},{12,... | collective-permute-start | bytes 6291464 | tf_op jit(solution)/shard_map/ppermute | solution.py:259
  213.9 66.2 %collective-permute-done.2 = bf16[64,64,256]{2,1,0:T(8,128)(2,1)} collective-permute-done((bf16[64,64,256]{2,1,0:T(8,128)(2,1)}, bf16[64,64,256]{2,1,0:T(8,128)(2,1)}, u32[]{:S(2)}, u32[]{:S(2)}) %collective-permute-start.2) | collective-permute-done | bytes 2097184 | tf_op jit(solution)/shard_map/ppermute | solution.py:259
  283.1 1.5 constant_dynamic-update-slice_fusion.12
  287.5 3.1 constant_dynamic-update-slice_fusion.7
  290.6 3.2 constant_dynamic-update-slice_fusion.6
  293.9 1.5 constant_dynamic-update-slice_fusion.5
  295.4 1.5 constant_dynamic-update-slice_fusion.4
  299.1 25.8 %collective-permute-done.6 = bf16[64,64,256]{2,1,0:T(8,128)(2,1)S(1)} collective-permute-done((bf16[64,64,256]{2,1,0:T(8,128)(2,1)}, bf16[64,64,256]{2,1,0:T(8,128)(2,1)S(1)}, u32[]{:S(2)}, u32[]{:S(2)}) %collective-permute-start.6) | collective-permute-done | bytes 2097184 | tf_op jit(solution)/shard_map/ppermute | solution.py:259
  326.4 21.2 %collective-permute-done.7 = bf16[64,64,256]{2,1,0:T(8,128)(2,1)S(1)} collective-permute-done((bf16[64,64,256]{2,1,0:T(8,128)(2,1)}, bf16[64,64,256]{2,1,0:T(8,128)(2,1)S(1)}, u32[]{:S(2)}, u32[]{:S(2)}) %collective-permute-start.7) | collective-permute-done | bytes 2097184 | tf_op jit(solution)/shard_map/ppermute | solution.py:259
  349.7 55.0 %advect.1 = bf16[64,64,256]{2,1,0:T(8,128)(2,1)} custom-call(s32[16,2]{1,0:T(8,128)S(1)} %copy.4.dep_ref, bf16[64,64,128]{2,1,0:T(8,128)(2,1)S(1)} %copy-done, bf16[516,64,256]{2,1,0:T(8,128)(2,1)} %constant_dynamic-update-slice_fusion.wt_ref, bf16[516,64,128]{2,1,0:T(8,128)(2,1)S(1)} %constant_dynamic-update-slice_fusion.10.ww_ref), custom_call_target="tpu_custom_call" | custom-call | tf_op jit(solution)/shard_map/advect/pallas_call | solution.py:227
  (48 shorter events, 17.9 us)
Async XLA Ops:
  0.0 67.6 %collective-permute-start.10 = (bf16[64,64,128]{2,1,0:T(8,128)(2,1)}, bf16[64,64,128]{2,1,0:T(8,128)(2,1)S(1)}, u32[]{:S(2)}, u32[]{:S(2)}) collective-permute-start(bf16[64,64,128]{2,1,0:T(8,128)(2,1)} %here_ref.1), channel_id=1, source_target_pairs={{13,0},{14,1},{15,2},{0,3},{1,4},{2,5},{3,6},{4,7},{5,8},{6,9},{7,... | collective-permute-start | bytes 3145736 | tf_op jit(solution)/shard_map/ppermute | solution.py:259
  2.4 69.3 %collective-permute-start.11 = (bf16[64,64,128]{2,1,0:T(8,128)(2,1)}, bf16[64,64,128]{2,1,0:T(8,128)(2,1)}, u32[]{:S(2)}, u32[]{:S(2)}) collective-permute-start(bf16[64,64,128]{2,1,0:T(8,128)(2,1)} %here_ref.1), channel_id=1, source_target_pairs={{14,0},{15,1},{0,2},{1,3},{2,4},{3,5},{4,6},{5,7},{6,8},{7,9},{8,1... | collective-permute-start | bytes 3145736 | tf_op jit(solution)/shard_map/ppermute | solution.py:259
  4.8 6.1 %collective-permute-start.9 = (bf16[2,64,128]{2,1,0:T(8,128)(2,1)S(1)}, bf16[2,64,128]{2,1,0:T(8,128)(2,1)S(1)}, u32[]{:S(2)}, u32[]{:S(2)}) collective-permute-start(bf16[2,64,128]{2,1,0:T(8,128)(2,1)S(1)} %get-tuple-element.8), channel_id=1, source_target_pairs={{12,0},{13,1},{14,2},{15,3},{0,4},{1,5},{2,6},{3,7},{4,8},{5,9},{6... | collective-permute-start | bytes 98312 | tf_op jit(solution)/shard_map/ppermute | solution.py:259
  6.3 67.9 %collective-permute-start.12 = (bf16[64,64,128]{2,1,0:T(8,128)(2,1)}, bf16[64,64,128]{2,1,0:T(8,128)(2,1)}, u32[]{:S(2)}, u32[]{:S(2)}) collective-permute-start(bf16[64,64,128]{2,1,0:T(8,128)(2,1)} %here_ref.1), channel_id=1, source_target_pairs={{15,0},{0,1},{1,2},{2,3},{3,4},{4,5},{5,6},{6,7},{7,8},{8,9},{9,10... | collective-permute-start | bytes 3145736 | tf_op jit(solution)/shard_map/ppermute | solution.py:259
  6.5 68.5 %collective-permute-start.13 = (bf16[64,64,128]{2,1,0:T(8,128)(2,1)}, bf16[64,64,128]{2,1,0:T(8,128)(2,1)S(1)}, u32[]{:S(2)}, u32[]{:S(2)}) collective-permute-start(bf16[64,64,128]{2,1,0:T(8,128)(2,1)} %here_ref.1), channel_id=1, source_target_pairs={{1,0},{2,1},{3,2},{4,3},{5,4},{6,5},{7,6},{8,7},{9,8},{10,9},{11,1... | collective-permute-start | bytes 3145736 | tf_op jit(solution)/shard_map/ppermute | solution.py:259
  10.8 44.5 %collective-permute-start.17 = (bf16[2,64,128]{2,1,0:T(8,128)(2,1)S(1)}, bf16[2,64,128]{2,1,0:T(8,128)(2,1)S(1)}, u32[]{:S(2)}, u32[]{:S(2)}) collective-permute-start(bf16[2,64,128]{2,1,0:T(8,128)(2,1)S(1)} %get-tuple-element.7), channel_id=1, source_target_pairs={{5,0},{6,1},{7,2},{8,3},{9,4},{10,5},{11,6},{12,7},{13,8},{14,9},{... | collective-permute-start | bytes 98312 | tf_op jit(solution)/shard_map/ppermute | solution.py:259
  55.3 6.1 %collective-permute-start = (bf16[2,64,256]{2,1,0:T(8,128)(2,1)S(1)}, bf16[2,64,256]{2,1,0:T(8,128)(2,1)S(1)}, u32[]{:S(2)}, u32[]{:S(2)}) collective-permute-start(bf16[2,64,256]{2,1,0:T(8,128)(2,1)S(1)} %get-tuple-element.6), channel_id=1, source_target_pairs={{12,0},{13,1},{14,2},{15,3},{0,4},{1,5},{2,6},{3,7},{4,8},{5,9},{6... | collective-permute-start | bytes 196616 | tf_op jit(solution)/shard_map/ppermute | solution.py:259
  61.4 151.0 %collective-permute-start.1 = (bf16[64,64,256]{2,1,0:T(8,128)(2,1)}, bf16[64,64,256]{2,1,0:T(8,128)(2,1)S(1)}, u32[]{:S(2)}, u32[]{:S(2)}) collective-permute-start(bf16[64,64,256]{2,1,0:T(8,128)(2,1)} %param.3), channel_id=1, source_target_pairs={{13,0},{14,1},{15,2},{0,3},{1,4},{2,5},{3,6},{4,7},{5,8},{6,9},{7,... | collective-permute-start | bytes 6291464 | tf_op jit(solution)/shard_map/ppermute | solution.py:259
  67.6 212.5 %collective-permute-start.2 = (bf16[64,64,256]{2,1,0:T(8,128)(2,1)}, bf16[64,64,256]{2,1,0:T(8,128)(2,1)}, u32[]{:S(2)}, u32[]{:S(2)}) collective-permute-start(bf16[64,64,256]{2,1,0:T(8,128)(2,1)} %param.3), channel_id=1, source_target_pairs={{14,0},{15,1},{0,2},{1,3},{2,4},{3,5},{4,6},{5,7},{6,8},{7,9},{8,1... | collective-permute-start | bytes 6291464 | tf_op jit(solution)/shard_map/ppermute | solution.py:259
  71.7 48.4 %collective-permute-start.14 = (bf16[64,64,128]{2,1,0:T(8,128)(2,1)}, bf16[64,64,128]{2,1,0:T(8,128)(2,1)S(1)}, u32[]{:S(2)}, u32[]{:S(2)}) collective-permute-start(bf16[64,64,128]{2,1,0:T(8,128)(2,1)} %here_ref.1), channel_id=1, source_target_pairs={{2,0},{3,1},{4,2},{5,3},{6,4},{7,5},{8,6},{9,7},{10,8},{11,9},{12,... | collective-permute-start | bytes 3145736 | tf_op jit(solution)/shard_map/ppermute | solution.py:259
  74.2 100.1 %collective-permute-start.15 = (bf16[64,64,128]{2,1,0:T(8,128)(2,1)}, bf16[64,64,128]{2,1,0:T(8,128)(2,1)}, u32[]{:S(2)}, u32[]{:S(2)}) collective-permute-start(bf16[64,64,128]{2,1,0:T(8,128)(2,1)} %here_ref.1), channel_id=1, source_target_pairs={{3,0},{4,1},{5,2},{6,3},{7,4},{8,5},{9,6},{10,7},{11,8},{12,9},{13... | collective-permute-start | bytes 3145736 | tf_op jit(solution)/shard_map/ppermute | solution.py:259
  75.0 57.9 %copy-start.2 = (bf16[64,64,128]{2,1,0:T(8,128)(2,1)}, bf16[64,64,128]{2,1,0:T(8,128)(2,1)S(1)}, u32[]{:S(2)}) copy-start(bf16[64,64,128]{2,1,0:T(8,128)(2,1)S(1)} %collective-permute-done.13) | copy-start | bytes 3145732
  75.0 113.7 %collective-permute-start.16 = (bf16[64,64,128]{2,1,0:T(8,128)(2,1)}, bf16[64,64,128]{2,1,0:T(8,128)(2,1)}, u32[]{:S(2)}, u32[]{:S(2)}) collective-permute-start(bf16[64,64,128]{2,1,0:T(8,128)(2,1)} %here_ref.1), channel_id=1, source_target_pairs={{4,0},{5,1},{6,2},{7,3},{8,4},{9,5},{10,6},{11,7},{12,8},{13,9},{1... | collective-permute-start | bytes 3145736 | tf_op jit(solution)/shard_map/ppermute | solution.py:259
  120.1 12.8 %copy-start.4 = (bf16[64,64,128]{2,1,0:T(8,128)(2,1)}, bf16[64,64,128]{2,1,0:T(8,128)(2,1)S(1)}, u32[]{:S(2)}) copy-start(bf16[64,64,128]{2,1,0:T(8,128)(2,1)S(1)} %collective-permute-done.14) | copy-start | bytes 3145732
  120.1 170.5 %collective-permute-start.3 = (bf16[64,64,256]{2,1,0:T(8,128)(2,1)}, bf16[64,64,256]{2,1,0:T(8,128)(2,1)}, u32[]{:S(2)}, u32[]{:S(2)}) collective-permute-start(bf16[64,64,256]{2,1,0:T(8,128)(2,1)} %param.3), channel_id=1, source_target_pairs={{15,0},{0,1},{1,2},{2,3},{3,4},{4,5},{5,6},{6,7},{7,8},{8,9},{9,10... | collective-permute-start | bytes 6291464 | tf_op jit(solution)/shard_map/ppermute | solution.py:259
  133.7 149.1 %copy-start.3 = (bf16[64,64,128]{2,1,0:T(8,128)(2,1)S(1)}, bf16[64,64,128]{2,1,0:T(8,128)(2,1)}, u32[]{:S(2)}) copy-start(bf16[64,64,128]{2,1,0:T(8,128)(2,1)} %copy-done.2) | copy-start | bytes 3145732
  133.7 149.2 %copy-start.5 = (bf16[64,64,128]{2,1,0:T(8,128)(2,1)S(1)}, bf16[64,64,128]{2,1,0:T(8,128)(2,1)}, u32[]{:S(2)}) copy-start(bf16[64,64,128]{2,1,0:T(8,128)(2,1)} %copy-done.4) | copy-start | bytes 3145732
  174.3 121.1 %collective-permute-start.4 = (bf16[64,64,256]{2,1,0:T(8,128)(2,1)}, bf16[64,64,256]{2,1,0:T(8,128)(2,1)S(1)}, u32[]{:S(2)}, u32[]{:S(2)}) collective-permute-start(bf16[64,64,256]{2,1,0:T(8,128)(2,1)} %param.3), channel_id=1, source_target_pairs={{1,0},{2,1},{3,2},{4,3},{5,4},{6,5},{7,6},{8,7},{9,8},{10,9},{11,1... | collective-permute-start | bytes 6291464 | tf_op jit(solution)/shard_map/ppermute | solution.py:259
  188.7 108.9 %collective-permute-start.5 = (bf16[64,64,256]{2,1,0:T(8,128)(2,1)}, bf16[64,64,256]{2,1,0:T(8,128)(2,1)S(1)}, u32[]{:S(2)}, u32[]{:S(2)}) collective-permute-start(bf16[64,64,256]{2,1,0:T(8,128)(2,1)} %param.3), channel_id=1, source_target_pairs={{2,0},{3,1},{4,2},{5,3},{6,4},{7,5},{8,6},{9,7},{10,8},{11,9},{12,... | collective-permute-start | bytes 6291464 | tf_op jit(solution)/shard_map/ppermute | solution.py:259
  212.4 112.6 %collective-permute-start.6 = (bf16[64,64,256]{2,1,0:T(8,128)(2,1)}, bf16[64,64,256]{2,1,0:T(8,128)(2,1)S(1)}, u32[]{:S(2)}, u32[]{:S(2)}) collective-permute-start(bf16[64,64,256]{2,1,0:T(8,128)(2,1)} %param.3), channel_id=1, source_target_pairs={{3,0},{4,1},{5,2},{6,3},{7,4},{8,5},{9,6},{10,7},{11,8},{12,9},{13... | collective-permute-start | bytes 6291464 | tf_op jit(solution)/shard_map/ppermute | solution.py:259
  280.1 67.6 %collective-permute-start.7 = (bf16[64,64,256]{2,1,0:T(8,128)(2,1)}, bf16[64,64,256]{2,1,0:T(8,128)(2,1)S(1)}, u32[]{:S(2)}, u32[]{:S(2)}) collective-permute-start(bf16[64,64,256]{2,1,0:T(8,128)(2,1)} %param.3), channel_id=1, source_target_pairs={{4,0},{5,1},{6,2},{7,3},{8,4},{9,5},{10,6},{11,7},{12,8},{13,9},{1... | collective-permute-start | bytes 6291464 | tf_op jit(solution)/shard_map/ppermute | solution.py:259
  283.1 10.7 %copy-start.1 = (bf16[64,64,256]{2,1,0:T(8,128)(2,1)S(1)}, bf16[64,64,256]{2,1,0:T(8,128)(2,1)}, u32[]{:S(2)}) copy-start(bf16[64,64,256]{2,1,0:T(8,128)(2,1)} %param.3) | copy-start | bytes 6291460
  290.6 58.4 %collective-permute-start.8 = (bf16[2,64,256]{2,1,0:T(8,128)(2,1)S(1)}, bf16[2,64,256]{2,1,0:T(8,128)(2,1)S(1)}, u32[]{:S(2)}, u32[]{:S(2)}) collective-permute-start(bf16[2,64,256]{2,1,0:T(8,128)(2,1)S(1)} %get-tuple-element.5), channel_id=1, source_target_pairs={{5,0},{6,1},{7,2},{8,3},{9,4},{10,5},{11,6},{12,7},{13,8},{14,9},{... | collective-permute-start | bytes 196616 | tf_op jit(solution)/shard_map/ppermute | solution.py:259
  295.4 54.3 %copy-start = (bf16[64,64,128]{2,1,0:T(8,128)(2,1)S(1)}, bf16[64,64,128]{2,1,0:T(8,128)(2,1)}, u32[]{:S(2)}) copy-start(bf16[64,64,128]{2,1,0:T(8,128)(2,1)} %here_ref.1) | copy-start | bytes 3145732

commit v2 on v1

--- a/solution.py
+++ b/solution.py
@@ -253,22 +253,212 @@
         name="advect",
     )(departures[0], wind_fields, wt, ww)
 
-def shifted(block, distance):
+def gather_kernel(columns, chunks, t_ref, w_ref, wt_ref, ww_ref, send, recv, edge_send, edge_recv, keep):
     count = lax.axis_size("lon")
-    route = [((i - distance) % count, i) for i in range(count)]
-    return lax.ppermute(block, "lon", route)
-
-
-def window(block):
-    pieces = [shifted(block[-2:], -LOW + 1)]
-    for offset in range(LOW, HIGH + 1):
-        pieces.append(block if offset == 0 else shifted(block, -offset))
-    pieces.append(shifted(block[:2], -HIGH - 1))
-    return jnp.concatenate(pieces, 0)
+    me = lax.axis_index("lon")
+    core = lax.rem(me, 2)
+    odd = lax.rem(me // 2, 2)
+    piece = columns // chunks
+    pairs = ((t_ref, wt_ref), (w_ref, ww_ref))
+
+    def device(distance):
+        return lax.rem(me + distance + count, count)
+
+    def landing(offset, q):
+        return pl.ds(2 + (offset - LOW) * columns + q * piece, piece)
+
+    def own(flow, q, distance):
+        return [
+            pltpu.make_async_remote_copy(
+                src_ref=local.at[pl.ds(q * piece, piece)],
+                dst_ref=far.at[landing(-distance, q)],
+                send_sem=send.at[flow, q, a],
+                recv_sem=recv.at[-distance - LOW, q, a],
+                device_id={"lon": device(distance)},
+                device_id_type=MESH,
+            )
+            for a, (local, far) in enumerate(pairs)
+        ]
+
+    def relay(flow, q, offset, distance):
+        return [
+            pltpu.make_async_remote_copy(
+                src_ref=far.at[landing(offset, q)],
+                dst_ref=far.at[landing(offset - distance, q)],
+                send_sem=send.at[flow, q, a],
+                recv_sem=recv.at[offset - distance - LOW, q, a],
+                device_id={"lon": device(distance)},
+                device_id_type=MESH,
+            )
+            for a, (_, far) in enumerate(pairs)
+        ]
+
+    def arrived(offset, q):
+        for a, (local, far) in enumerate(pairs):
+            pltpu.make_async_remote_copy(
+                src_ref=local.at[pl.ds(0, piece)],
+                dst_ref=far.at[landing(offset, q)],
+                send_sem=send.at[0, q, a],
+                recv_sem=recv.at[offset - LOW, q, a],
+                device_id={"lon": device(1)},
+                device_id_type=MESH,
+            ).wait_recv()
+
+    def edges():
+        out = []
+        for a, (local, far) in enumerate(pairs):
+            size = (HIGH - LOW + 1) * columns
+            for side, (source, target, distance) in enumerate(
+                ((columns - 2, 0, 1 - LOW), (0, 2 + size, -1 - HIGH))
+            ):
+                out.append(
+                    pltpu.make_async_remote_copy(
+                        src_ref=local.at[pl.ds(source, 2)],
+                        dst_ref=far.at[pl.ds(target, 2)],
+                        send_sem=edge_send.at[side, a],
+                        recv_sem=edge_recv.at[side, a],
+                        device_id={"lon": device(distance)},
+                        device_id_type=MESH,
+                    )
+                )
+        return out
+
+    def stay():
+        return [
+            pltpu.make_async_copy(local, far.at[pl.ds(2 - LOW * columns, columns)], keep.at[a])
+            for a, (local, far) in enumerate(pairs)
+        ]
+
+    sibling = 1 - 2 * core
+    across = 2 - 4 * odd
+
+    barrier = pltpu.get_barrier_semaphore()
+    reach = 1 + HIGH
+    for distance in range(1, reach + 1):
+        for way in (distance, -distance):
+            pl.semaphore_signal(
+                barrier, inc=1, device_id={"lon": device(way)}, device_id_type=MESH
+            )
+    pl.semaphore_wait(barrier, 2 * reach)
+
+    def begin(copies):
+        for c in copies:
+            c.start()
+
+    def end(copies):
+        for c in copies:
+            c.wait_send()
+
+    passes_on = (1 - odd) + odd * core
+
+    def first(q, carry):
+        begin(own(1, q, across))
+        begin(own(2, q, -4))
+
+        @pl.when(core == 1)
+        def _():
+            begin(own(3, q, 3))
+
+        begin(own(0, q, sibling))
+        return carry
+
+    lax.fori_loop(0, chunks, first, 0)
+    begin(edges())
+    begin(stay())
+
+    def late(q):
+        arrived(-across, q)
+        begin(relay(7, q, -across, sibling))
+
+    def step(q, carry):
+        arrived(across, q)
+
+        @pl.when(passes_on == 1)
+        def _():
+            begin(relay(4, q, across, 2 * across))
+
+        begin(relay(5, q, across, sibling))
+        arrived(4, q)
+
+        @pl.when(core == 0)
+        def _():
+            @pl.when(odd == 0)
+            def _():
+                begin(relay(8, q, 4, 2))
+
+            begin(relay(6, q, 4, sibling))
+
+        @pl.when(q > 0)
+        def _():
+            late(q - 1)
+
+        return carry
+
+    lax.fori_loop(0, chunks, step, 0)
+    late(chunks - 1)
+
+    def finish(q, carry):
+        for offset in (-3, -1, 1, 3):
+            arrived(offset, q)
+        end(own(0, q, sibling))
+        end(own(1, q, across))
+        end(own(2, q, -4))
+
+        @pl.when(core == 1)
+        def _():
+            end(own(3, q, 3))
+
+        @pl.when(passes_on == 1)
+        def _():
+            end(relay(4, q, across, 2 * across))
+
+        end(relay(5, q, across, sibling))
+
+        @pl.when(core == 0)
+        def _():
+            @pl.when(odd == 0)
+            def _():
+                end(relay(8, q, 4, 2))
+
+            end(relay(6, q, 4, sibling))
+
+        end(relay(7, q, -across, sibling))
+        return carry
+
+    lax.fori_loop(0, chunks, finish, 0)
+    for c in edges():
+        c.wait()
+    for c in stay():
+        c.wait()
+
+
+def gather_window(tracers, wind_fields):
+    columns = tracers.shape[0]
+    long = (HIGH - LOW + 1) * columns + 4
+    shapes = [jax.ShapeDtypeStruct((long,) + x.shape[1:], x.dtype) for x in (tracers, wind_fields)]
+    dma = pltpu.SemaphoreType.DMA
+    return pl.pallas_call(
+        functools.partial(gather_kernel, columns, CHUNKS),
+        out_shape=shapes,
+        in_specs=[pl.BlockSpec(memory_space=pl.ANY)] * 2,
+        out_specs=[pl.BlockSpec(memory_space=pl.ANY)] * 2,
+        scratch_shapes=[
+            dma((9, CHUNKS, 2)),
+            dma((HIGH - LOW + 1, CHUNKS, 2)),
+            dma((2, 2)),
+            dma((2, 2)),
+            dma((2,)),
+        ],
+        compiler_params=pltpu.CompilerParams(
+            collective_id=0, has_side_effects=True, vmem_limit_bytes=1024 * 1024
+        ),
+        name="gather_window",
+    )(tracers, wind_fields)
 
 
 def on_device(tracers, wind_fields, departures):
-    return advect(tracers.shape, wind_fields, departures, window(tracers), window(wind_fields))
+    wt, ww = gather_window(tracers, wind_fields)
+    return advect(tracers.shape, wind_fields, departures, wt, ww)
 
 
 def solution(mesh):

time: 405 us -> 250 us (0.62)
  waiting for transfers between devices: 205 us -> 0 us
  Pallas kernels: 55 us -> 239 us
  starting transfers between devices: 118 us -> 0 us
  local copies, waits for them, and re-layouts: 26.3 us -> 10.6 us
    ppermute x18 -> x0, waiting for transfers between devices: 205 us -> none  [shifted(): return lax.ppermute(block, 'lon', route)]
    pallas_call x0 -> x1, Pallas kernels: none -> 184 us  [gather_window(): pl.pallas_call(functools.partial(gather_kernel, columns, CHUNKS), out_sha...]
    ppermute x18 -> x0, starting transfers between devices: 118 us -> none  [shifted(): return lax.ppermute(block, 'lon', route)]
    unnamed x30 -> x8, local copies, waits for them, and re-layouts: 23.2 us -> 9.81 us
  transfers between devices with their start and end apart: 18 -> 0, of which waited for: 8 -> 0; matrix products, arithmetic and copies ran while one was open for 6% -> 0% of each run, Pallas kernels for 0% -> 0%
where the time goes in v2:
time: 250 us
  Pallas kernels  239 us (96%)
  local copies, waits for them, and re-layouts  10.6 us (4%)
    pallas_call x1, Pallas kernels, gather_window(): pl.pallas_call(functools.partial(gather_kernel, columns, CHUNKS), out_sha...  184 us
    pallas_call x1, Pallas kernels, advect(): pl.pallas_call(functools.partial(advect_kernel, columns, rows, levels), o...  55 us
    unnamed x8, local copies, waits for them, and re-layouts  9.81 us

profile of v2, /device:TPU:0, one launch (start us, length us, event | category | flops | bytes accessed | tf_op | source)
XLA Modules:
  0.0 249.6 jit_solution(18189032206070069153)
XLA Ops:
  0.0 0.8 copy.4.dep_ref
  0.8 0.0 copy-start.1
  0.8 1.2 copy-done.1
  2.0 0.0 copy-start.3
  2.0 1.6 copy-done.3
  3.6 184.0 %gather_window.1 = (bf16[516,64,256]{2,1,0:T(8,128)(2,1)S(1)}, bf16[516,64,128]{2,1,0:T(8,128)(2,1)S(1)}) custom-call(bf16[64,64,256]{2,1,0:T(8,128)(2,1)S(1)} %copy-done.3, bf16[64,64,128]{2,1,0:T(8,128)(2,1)S(1)} %copy-done.1), custom_call_target="tpu_custom_call" | custom-call | tf_op jit(solution)/shard_map/gather_window/pallas_call | solution.py:440
  187.5 0.0 copy-start
  187.5 5.8 %copy-done = bf16[516,64,256]{2,1,0:T(8,128)(2,1)} copy-done((bf16[516,64,256]{2,1,0:T(8,128)(2,1)}, bf16[516,64,256]{2,1,0:T(8,128)(2,1)S(1)}, u32[]{:S(2)}) %copy-start) | copy-done | bytes 16908312
  193.3 0.0 copy-start.2
  193.3 1.2 copy-done.2
  194.5 55.0 %advect.1 = bf16[64,64,256]{2,1,0:T(8,128)(2,1)} custom-call(s32[16,2]{1,0:T(8,128)S(1)} %copy.4.dep_ref, bf16[64,64,128]{2,1,0:T(8,128)(2,1)S(1)} %copy-done.2, bf16[516,64,256]{2,1,0:T(8,128)(2,1)} %copy-done, bf16[516,64,128]{2,1,0:T(8,128)(2,1)S(1)} %get-tuple-element.8.ww_ref), custom_call_target="tpu_custom_call" | custom-call | tf_op jit(solution)/shard_map/advect/pallas_call | solution.py:227
Async XLA Ops:
  0.8 1.2 copy-start.1
  2.0 1.6 copy-start.3
  187.5 5.8 %copy-start = (bf16[516,64,256]{2,1,0:T(8,128)(2,1)}, bf16[516,64,256]{2,1,0:T(8,128)(2,1)S(1)}, u32[]{:S(2)}) copy-start(bf16[516,64,256]{2,1,0:T(8,128)(2,1)S(1)} %get-tuple-element.7.wt_ref) | copy-start | bytes 50724868
  193.3 1.2 copy-start.2

commit v3 on v2

--- a/solution.py
+++ b/solution.py
@@ -249,7 +249,7 @@
                 pltpu.SemaphoreType.DMA((2, 2, 2)),
             ],
         ),
-        compiler_params=pltpu.CompilerParams(vmem_limit_bytes=40 * 1024 * 1024),
+        compiler_params=pltpu.CompilerParams(vmem_limit_bytes=60 * 1024 * 1024),
         name="advect",
     )(departures[0], wind_fields, wt, ww)
 
@@ -349,7 +349,8 @@
         for c in copies:
             c.wait_send()
 
-    passes_on = (1 - odd) + odd * core
+    passes_on = (1 - odd) * (1 - core)
+    turns_back = odd * (1 - core)
 
     def first(q, carry):
         begin(own(1, q, across))
@@ -380,13 +381,18 @@
         begin(relay(5, q, across, sibling))
         arrived(4, q)
 
+        @pl.when(odd == 0)
+        def _():
+            begin(relay(8, q, 4, 2))
+
         @pl.when(core == 0)
         def _():
-            @pl.when(odd == 0)
-            def _():
-                begin(relay(8, q, 4, 2))
-
             begin(relay(6, q, 4, sibling))
+
+        @pl.when(turns_back == 1)
+        def _():
+            arrived(-3, q)
+            begin(relay(3, q, -3, -1))
 
         @pl.when(q > 0)
         def _():
@@ -398,7 +404,7 @@
     late(chunks - 1)
 
     def finish(q, carry):
-        for offset in (-3, -1, 1, 3):
+        for offset in (-1, 1, 3):
             arrived(offset, q)
         end(own(0, q, sibling))
         end(own(1, q, across))
@@ -414,13 +420,21 @@
 
         end(relay(5, q, across, sibling))
 
+        @pl.when(odd == 0)
+        def _():
+            end(relay(8, q, 4, 2))
+
         @pl.when(core == 0)
         def _():
-            @pl.when(odd == 0)
-            def _():
-                end(relay(8, q, 4, 2))
-
             end(relay(6, q, 4, sibling))
+
+        @pl.when(turns_back == 1)
+        def _():
+            end(relay(3, q, -3, -1))
+
+        @pl.when(turns_back == 0)
+        def _():
+            arrived(-3, q)
 
         end(relay(7, q, -across, sibling))
         return carry
@@ -449,9 +463,7 @@
             dma((2, 2)),
             dma((2,)),
         ],
-        compiler_params=pltpu.CompilerParams(
-            collective_id=0, has_side_effects=True, vmem_limit_bytes=1024 * 1024
-        ),
+        compiler_params=pltpu.CompilerParams(collective_id=0, has_side_effects=True),
         name="gather_window",
     )(tracers, wind_fields)
 

time: 250 us -> 208 us (0.83)
  Pallas kernels: 239 us -> 207 us
  local copies, waits for them, and re-layouts: 10.6 us -> 1.35 us
    pallas_call x1, Pallas kernels: 184 us -> 151 us  [gather_window(): pl.pallas_call(functools.partial(gather_kernel, columns, CHUNKS), out_sha...]
    unnamed x8 -> x0, local copies, waits for them, and re-layouts: 9.81 us -> none
where the time goes in v3:
time: 208 us
  Pallas kernels  207 us (100%)
    pallas_call x1, Pallas kernels, gather_window(): pl.pallas_call(functools.partial(gather_kernel, columns, CHUNKS), out_sha...  151 us
    pallas_call x1, Pallas kernels, advect(): pl.pallas_call(functools.partial(advect_kernel, columns, rows, levels), o...  55.5 us

profile of v3, /device:TPU:0, one launch (start us, length us, event | category | flops | bytes accessed | tf_op | source)
XLA Modules:
  0.0 208.1 jit_solution(1617330943807689622)
XLA Ops:
  0.0 1.3 copy.4.dep_ref
  1.3 151.2 %gather_window.1 = (bf16[516,64,256]{2,1,0:T(8,128)(2,1)}, bf16[516,64,128]{2,1,0:T(8,128)(2,1)}) custom-call(bf16[64,64,256]{2,1,0:T(8,128)(2,1)} %t_ref.1, bf16[64,64,128]{2,1,0:T(8,128)(2,1)} %here_ref.1), custom_call_target="tpu_custom_call" | custom-call | tf_op jit(solution)/shard_map/gather_window/pallas_call | solution.py:454
  152.6 55.5 %advect.1 = bf16[64,64,256]{2,1,0:T(8,128)(2,1)} custom-call(s32[16,2]{1,0:T(8,128)} %copy.4.dep_ref, bf16[64,64,128]{2,1,0:T(8,128)(2,1)} %here_ref.1, bf16[516,64,256]{2,1,0:T(8,128)(2,1)} %get-tuple-element.7.wt_ref, bf16[516,64,128]{2,1,0:T(8,128)(2,1)} %get-tuple-element.8.ww_ref), custom_call_target="tpu_custom_call" | custom-call | tf_op jit(solution)/shard_map/advect/pallas_call | solution.py:227

commit v4 on v3

--- a/solution.py
+++ b/solution.py
@@ -11,7 +11,7 @@
 TRAJ = 3
 CLIP_BOUND = 0.95
 LOW, HIGH = -3, 4
-CHUNKS = 8
+CHUNKS = 16
 MESH = pl.DeviceIdType.MESH
 
 
@@ -124,13 +124,13 @@
             yield k, (pltpu.roll(e, 8 - k, a.ndim - 2) if k else e)
 
     def build(i, carry):
-        for u in range(2):
-            col = i * 2 + u
+        for u in range(4):
+            col = i * 4 + u
             for k, value in interleave(t8[0, col], t8[1, col], range(5)):
                 s_ref[k, col] = value
         return carry
 
-    lax.fori_loop(0, width // 2, build, 0)
+    lax.fori_loop(0, width // 4, build, 0)
 
     def packed_ext(j, col):
         low = w8[j, col]
@@ -186,8 +186,8 @@
             both, e_ref[:, at], preferred_element_type=jnp.float32
         ).reshape(half, 8, tracer_ch)
 
-    def interpolate(i, carry):
-        for h in range(2):
+    def interpolate(step, carry):
+        for i, h in ((2 * step, 0), (2 * step, 1), (2 * step + 1, 0), (2 * step + 1, 1)):
             for v in range(lane_tiles):
                 lanes = slice(v * 128, (v + 1) * 128)
                 re = r_ref[i, :, (2 * h) * tracer_ch + v * 128 : (2 * h) * tracer_ch + (v + 1) * 128]
@@ -213,7 +213,7 @@
                 out_ref[i + half * h, :, lanes] = acc.astype(out_ref.dtype)
         return carry
 
-    lax.fori_loop(0, half, interpolate, 0)
+    lax.fori_loop(0, half // 2, interpolate, 0)
 
 
 def advect(tracers_shape, wind_fields, departures, wt, ww):
@@ -253,7 +253,8 @@
         name="advect",
     )(departures[0], wind_fields, wt, ww)
 
-def gather_kernel(columns, chunks, t_ref, w_ref, wt_ref, ww_ref, send, recv, edge_send, edge_recv, keep):
+def gather_kernel(columns, chunks, t_ref, w_ref, wt_ref, ww_ref,
+                  spill_t, spill_w, send, recv, spill_recv, edge_send, edge_recv, keep):
     count = lax.axis_size("lon")
     me = lax.axis_index("lon")
     core = lax.rem(me, 2)
@@ -303,6 +304,34 @@
                 device_id={"lon": device(1)},
                 device_id_type=MESH,
             ).wait_recv()
+
+    spills = (spill_t, spill_w)
+
+    def detour(q):
+        return [
+            pltpu.make_async_remote_copy(
+                src_ref=local.at[pl.ds(q * piece, piece)],
+                dst_ref=spills[a].at[pl.ds(q * piece, piece)],
+                send_sem=send.at[3, q, a],
+                recv_sem=spill_recv.at[q, a],
+                device_id={"lon": device(4)},
+                device_id_type=MESH,
+            )
+            for a, (local, _) in enumerate(pairs)
+        ]
+
+    def rejoin(q):
+        return [
+            pltpu.make_async_remote_copy(
+                src_ref=spills[a].at[pl.ds(q * piece, piece)],
+                dst_ref=far.at[landing(-2, q)],
+                send_sem=send.at[4, q, a],
+                recv_sem=recv.at[-2 - LOW, q, a],
+                device_id={"lon": device(-2)},
+                device_id_type=MESH,
+            )
+            for a, (_, far) in enumerate(pairs)
+        ]
 
     def edges():
         out = []
@@ -349,8 +378,16 @@
         for c in copies:
             c.wait_send()
 
-    passes_on = (1 - odd) * (1 - core)
     turns_back = odd * (1 - core)
+
+    def other(q):
+        return (2 - lax.rem(q, 3)) // 2
+
+    def passes_on(q):
+        return (1 - odd) * (1 - core) * (1 - other(q)) + odd * core * other(q)
+
+    def crosses(q):
+        return (1 - odd) * (1 - core * other(q))
 
     def first(q, carry):
         begin(own(1, q, across))
@@ -360,6 +397,10 @@
         def _():
             begin(own(3, q, 3))
 
+        @pl.when(turns_back * other(q) == 1)
+        def _():
+            begin(detour(q))
+
         begin(own(0, q, sibling))
         return carry
 
@@ -374,14 +415,14 @@
     def step(q, carry):
         arrived(across, q)
 
-        @pl.when(passes_on == 1)
+        @pl.when(passes_on(q) == 1)
         def _():
             begin(relay(4, q, across, 2 * across))
 
         begin(relay(5, q, across, sibling))
         arrived(4, q)
 
-        @pl.when(odd == 0)
+        @pl.when(crosses(q) == 1)
         def _():
             begin(relay(8, q, 4, 2))
 
@@ -392,7 +433,13 @@
         @pl.when(turns_back == 1)
         def _():
             arrived(-3, q)
-            begin(relay(3, q, -3, -1))
+            begin(relay(9, q, -3, -1))
+
+        @pl.when(turns_back * other(q) == 1)
+        def _():
+            for c in detour(q):
+                c.wait_recv()
+            begin(rejoin(q))
 
         @pl.when(q > 0)
         def _():
@@ -414,13 +461,13 @@
         def _():
             end(own(3, q, 3))
 
-        @pl.when(passes_on == 1)
+        @pl.when(passes_on(q) == 1)
         def _():
             end(relay(4, q, across, 2 * across))
 
         end(relay(5, q, across, sibling))
 
-        @pl.when(odd == 0)
+        @pl.when(crosses(q) == 1)
         def _():
             end(relay(8, q, 4, 2))
 
@@ -430,7 +477,12 @@
 
         @pl.when(turns_back == 1)
         def _():
-            end(relay(3, q, -3, -1))
+            end(relay(9, q, -3, -1))
+
+        @pl.when(turns_back * other(q) == 1)
+        def _():
+            end(detour(q))
+            end(rejoin(q))
 
         @pl.when(turns_back == 0)
         def _():
@@ -457,8 +509,11 @@
         in_specs=[pl.BlockSpec(memory_space=pl.ANY)] * 2,
         out_specs=[pl.BlockSpec(memory_space=pl.ANY)] * 2,
         scratch_shapes=[
-            dma((9, CHUNKS, 2)),
+            pltpu.VMEM(tracers.shape, tracers.dtype),
+            pltpu.VMEM(wind_fields.shape, wind_fields.dtype),
+            dma((10, CHUNKS, 2)),
             dma((HIGH - LOW + 1, CHUNKS, 2)),
+            dma((CHUNKS, 2)),
             dma((2, 2)),
             dma((2, 2)),
             dma((2,)),

time: 208 us -> 210 us (level)
  the two profiles are of different devices: /device:TPU:0 before, /device:TPU:23 now
where the time goes in v4:
time: 210 us
  Pallas kernels  208 us (99%)
    pallas_call x1, Pallas kernels, gather_window(): pl.pallas_call(functools.partial(gather_kernel, columns, CHUNKS), out_sha...  155 us
    pallas_call x1, Pallas kernels, advect(): pl.pallas_call(functools.partial(advect_kernel, columns, rows, levels), o...  53.1 us

profile of v4, /device:TPU:23, one launch (start us, length us, event | category | flops | bytes accessed | tf_op | source)
XLA Modules:
  0.0 209.6 jit_solution(12599389843098220915)
XLA Ops:
  0.0 1.3 copy.4.dep_ref
  1.3 155.2 %gather_window.1 = (bf16[516,64,256]{2,1,0:T(8,128)(2,1)}, bf16[516,64,128]{2,1,0:T(8,128)(2,1)}) custom-call(bf16[64,64,256]{2,1,0:T(8,128)(2,1)} %t_ref.1, bf16[64,64,128]{2,1,0:T(8,128)(2,1)} %here_ref.1), custom_call_target="tpu_custom_call" | custom-call | tf_op jit(solution)/shard_map/gather_window/pallas_call | solution.py:506
  156.5 53.1 %advect.1 = bf16[64,64,256]{2,1,0:T(8,128)(2,1)} custom-call(s32[16,2]{1,0:T(8,128)} %copy.4.dep_ref, bf16[64,64,128]{2,1,0:T(8,128)(2,1)} %here_ref.1, bf16[516,64,256]{2,1,0:T(8,128)(2,1)} %get-tuple-element.7.wt_ref, bf16[516,64,128]{2,1,0:T(8,128)(2,1)} %get-tuple-element.8.ww_ref), custom_call_target="tpu_custom_call" | custom-call | tf_op jit(solution)/shard_map/advect/pallas_call | solution.py:227

commit v5 on v4

--- a/solution.py
+++ b/solution.py
@@ -12,6 +12,8 @@
 CLIP_BOUND = 0.95
 LOW, HIGH = -3, 4
 CHUNKS = 16
+AHEAD = 4
+LAG = 2
 MESH = pl.DeviceIdType.MESH
 
 
@@ -404,7 +406,7 @@
         begin(own(0, q, sibling))
         return carry
 
-    lax.fori_loop(0, chunks, first, 0)
+    lax.fori_loop(0, AHEAD, first, 0)
     begin(edges())
     begin(stay())
 
@@ -441,14 +443,19 @@
                 c.wait_recv()
             begin(rejoin(q))
 
-        @pl.when(q > 0)
-        def _():
-            late(q - 1)
+        @pl.when(q >= LAG)
+        def _():
+            late(q - LAG)
+
+        @pl.when(q + AHEAD < chunks)
+        def _():
+            first(q + AHEAD, 0)
 
         return carry
 
     lax.fori_loop(0, chunks, step, 0)
-    late(chunks - 1)
+    for left in range(LAG, 0, -1):
+        late(chunks - left)
 
     def finish(q, carry):
         for offset in (-1, 1, 3):

time: 210 us -> 203 us (0.967)
  the two profiles are of different devices: /device:TPU:23 before, /device:TPU:0 now
where the time goes in v5:
time: 203 us
  Pallas kernels  202 us (100%)
    pallas_call x1, Pallas kernels, gather_window(): pl.pallas_call(functools.partial(gather_kernel, columns, CHUNKS), out_sha...  148 us
    pallas_call x1, Pallas kernels, advect(): pl.pallas_call(functools.partial(advect_kernel, columns, rows, levels), o...  53.1 us

profile of v5, /device:TPU:0, one launch (start us, length us, event | category | flops | bytes accessed | tf_op | source)
XLA Modules:
  0.0 202.9 jit_solution(10140995651549825663)
XLA Ops:
  0.0 1.3 copy.4.dep_ref
  1.3 148.4 %gather_window.1 = (bf16[516,64,256]{2,1,0:T(8,128)(2,1)}, bf16[516,64,128]{2,1,0:T(8,128)(2,1)}) custom-call(bf16[64,64,256]{2,1,0:T(8,128)(2,1)} %t_ref.1, bf16[64,64,128]{2,1,0:T(8,128)(2,1)} %here_ref.1), custom_call_target="tpu_custom_call" | custom-call | tf_op jit(solution)/shard_map/gather_window/pallas_call | solution.py:513
  149.7 53.1 %advect.1 = bf16[64,64,256]{2,1,0:T(8,128)(2,1)} custom-call(s32[16,2]{1,0:T(8,128)} %copy.4.dep_ref, bf16[64,64,128]{2,1,0:T(8,128)(2,1)} %here_ref.1, bf16[516,64,256]{2,1,0:T(8,128)(2,1)} %get-tuple-element.7.wt_ref, bf16[516,64,128]{2,1,0:T(8,128)(2,1)} %get-tuple-element.8.ww_ref), custom_call_target="tpu_custom_call" | custom-call | tf_op jit(solution)/shard_map/advect/pallas_call | solution.py:229

commit v6 on v5

--- a/solution.py
+++ b/solution.py
@@ -12,8 +12,8 @@
 CLIP_BOUND = 0.95
 LOW, HIGH = -3, 4
 CHUNKS = 16
-AHEAD = 4
-LAG = 2
+AHEAD = 16
+LAG = 8
 MESH = pl.DeviceIdType.MESH
 
 

time: 203 us -> 198 us (0.975)
  the two profiles are of different devices: /device:TPU:0 before, /device:TPU:29 now
where the time goes in v6:
time: 198 us
  Pallas kernels  196 us (99%)
    pallas_call x1, Pallas kernels, gather_window(): pl.pallas_call(functools.partial(gather_kernel, columns, CHUNKS), out_sha...  143 us
    pallas_call x1, Pallas kernels, advect(): pl.pallas_call(functools.partial(advect_kernel, columns, rows, levels), o...  53.2 us

profile of v6, /device:TPU:29, one launch (start us, length us, event | category | flops | bytes accessed | tf_op | source)
XLA Modules:
  0.0 197.7 jit_solution(10457809817619698328)
XLA Ops:
  0.0 1.3 copy.4.dep_ref
  1.3 143.2 %gather_window.1 = (bf16[516,64,256]{2,1,0:T(8,128)(2,1)}, bf16[516,64,128]{2,1,0:T(8,128)(2,1)}) custom-call(bf16[64,64,256]{2,1,0:T(8,128)(2,1)} %t_ref.1, bf16[64,64,128]{2,1,0:T(8,128)(2,1)} %here_ref.1), custom_call_target="tpu_custom_call" | custom-call | tf_op jit(solution)/shard_map/gather_window/pallas_call | solution.py:513
  144.5 53.2 %advect.1 = bf16[64,64,256]{2,1,0:T(8,128)(2,1)} custom-call(s32[16,2]{1,0:T(8,128)} %copy.4.dep_ref, bf16[64,64,128]{2,1,0:T(8,128)(2,1)} %here_ref.1, bf16[516,64,256]{2,1,0:T(8,128)(2,1)} %get-tuple-element.7.wt_ref, bf16[516,64,128]{2,1,0:T(8,128)(2,1)} %get-tuple-element.8.ww_ref), custom_call_target="tpu_custom_call" | custom-call | tf_op jit(solution)/shard_map/advect/pallas_call | solution.py:229
